TPU v7x, 512 devices: a whole 4x8x8 slice. The times are simulated.
512 devices in a mesh: box: 64 (over y, z), tile: 4 (over x_lo, core), col: 2 (over x_hi).
Axes of the slice: x: 4 (x_hi: 2, x_lo: 2; x = x_hi * 2 + x_lo), y: 8, z: 8, core: 2. Of those that a mesh axis runs over, the one named last changes fastest.
Arguments:
- box_operators: float32 [4, 64, 2, 256, 512], P(None, 'box', None, 'tile', 'col'), as said below
Outputs:
- merged: float32 [4, 64, 128, 512], P(None, 'box', 'tile', 'col')
Inputs may be any that keep to these rules, and one draw needn't show every extreme that they name: `box_operators`: every box's operator is symmetric and positive definite.
All inputs are finite; a program needn't handle non-finite values.
Results may differ from a plain program's by a relative error of at most 0.0001.
Values sent between devices are 32-bit elements; how exact they have to be, the bound alone decides.
A program may use at most 64 MiB of HBM per device.

v0:
```python
import jax
import jax.numpy as jnp
from jax import lax
from jax.sharding import PartitionSpec as P


def from_partner(block, axis, bit):
    count = lax.axis_size(axis)
    route = []
    for low in range(count):
        high = low | 1 << bit
        if high != low and high < count:
            route += [(low, high), (high, low)]
    return lax.ppermute(block, axis, route)


def gather_rows(stacked, level, half):
    whole = lax.all_gather(stacked, "tile", axis=2, tiled=True)
    if level == 1:
        return whole
    count = lax.axis_size("tile")
    split = whole.reshape(whole.shape[0], 2, count, whole.shape[2] // count, whole.shape[3])
    other = from_partner(split, "box", 0)
    joined = jnp.where(half == 0, jnp.stack([split, other], 3), jnp.stack([other, split], 3))
    return joined.reshape(whole.shape[0], 2, whole.shape[2] * 2, whole.shape[3])


def merge(tiles, side, bit, level, half):
    column = lax.axis_index("col")
    other = from_partner(tiles, "col", 0)
    blocks = jnp.where(column == 0, jnp.stack([tiles, other], 2), jnp.stack([other, tiles], 2))
    own_face = jnp.where(side == 0, blocks[:, 1], blocks[:, 0])
    whole = gather_rows(own_face, level, half)
    across = from_partner(whole, "box", bit)
    left = jnp.where(side == 0, whole, across)
    right = jnp.where(side == 0, across, whole)
    system = left[:, 1] + right[:, 0]
    target = jnp.where(column == 0, left[:, 0], right[:, 1])
    factor = jnp.linalg.cholesky(system)
    solved = jax.scipy.linalg.cho_solve((factor, True), target)
    coupling = jnp.where(side == 0, blocks[:, 0, 1], blocks[:, 1, 0])
    direct = jnp.where(side == 0, blocks[:, 0, 0], blocks[:, 1, 1])
    direct = jnp.where(column == side, direct, jnp.zeros_like(direct))
    return direct - jnp.einsum("brk,bkn->brn", coupling, solved, precision=lax.Precision.HIGHEST)


def per_device(box_operators):
    tiles = box_operators[:, 0]
    place = lax.axis_index("box")
    first = place % 2
    second = place // 2 % 2
    parent = merge(tiles, first, 0, 1, first)
    middle = parent.shape[1] // 2
    lower_half = parent[:, :middle]
    upper_half = parent[:, middle:]
    sent = jnp.where(first == 0, upper_half, lower_half)
    received = from_partner(sent, "box", 0)
    kept = jnp.where(first == 0, lower_half, upper_half)
    relaid = jnp.where(first == 0, jnp.stack([kept, received], 1), jnp.stack([received, kept], 1))
    grand = merge(relaid, second, 1, 2, first)
    return grand[:, None]


def solution(mesh):
    return jax.shard_map(
        per_device,
        mesh=mesh,
        in_specs=(P(None, "box", None, "tile", "col"),),
        out_specs=P(None, "box", "tile", "col"),
        check_vma=False,
    )
```

profile of v0, /device:TPU:1, one launch (start us, length us, event | category | flops | bytes accessed | tf_op | source)
XLA Modules:
  0.0 770.5 jit_solution(1618626363786046532)
XLA Ops:
  6.5 5.5 collective-permute-start
  13.1 7.3 collective-permute-done
  21.9 43.8 %all-gather.5.cloned.1.call-done = f32[4,1,2,256,256]{4,0,2,1,3:T(4,128)} async-done(((f32[4,1,2,64,256]{4,0,2,1,3:T(4,128)}), f32[4,1,2,256,256]{4,0,2,1,3:T(4,128)}) %all-gather.5.cloned.1.call-update) | async-done | bytes 2097168 | tf_op jit(solution)/shard_map/all_gather | solution.py:18
  67.6 3.3 collective-permute-start.1
  71.0 45.8 %collective-permute-done.1 = f32[4,2,256,256]{2,3,0,1:T(8,128)} collective-permute-done((f32[4,2,256,256]{2,3,0,1:T(8,128)S(1)}, f32[4,2,256,256]{2,3,0,1:T(8,128)}, u32[]{:S(2)}, u32[]{:S(2)}) %collective-permute-start.1) | collective-permute-done | bytes 2097184 | tf_op jit(solution)/shard_map/ppermute | solution.py:14
  126.8 47.2 %custom-call.19 = f32[4,128,128]{2,1,0:T(8,128)S(1)} custom-call(f32[4,128,128]{2,1,0:T(8,128)S(1)} %cholesky.198), custom_call_target="Cholesky" | custom-call | tf_op jit(solution)/shard_map/jit(cholesky)/cholesky | solution.py:39
  174.1 39.3 %custom-call.20 = f32[4,1,128,128]{2,3,1,0:T(8,128)S(1)} custom-call(f32[4,1,128,128]{3,2,1,0:T(8,128)S(1)} %select_bitcast_fusion.1), custom_call_target="InvertDiagBlocksLowerTriangular" | custom-call | tf_op jit(solution)/shard_map/jit(cholesky)/cholesky | solution.py:39
  216.4 46.9 %custom-call.21 = f32[4,128,128]{2,1,0:T(8,128)S(1)} custom-call(f32[4,128,128]{2,1,0:T(8,128)S(1)} %convolution_subtract_fusion.3), custom_call_target="Cholesky" | custom-call | tf_op jit(solution)/shard_map/jit(cholesky)/cholesky | solution.py:39
  263.9 4.1 while.4
  267.9 79.1 %custom-call.22 = f32[4,2,128,128]{2,3,1,0:T(8,128)S(1)} custom-call(f32[4,2,128,128]{3,2,1,0:T(8,128)S(1)} %bitcast.148), custom_call_target="InvertDiagBlocksLowerTriangular" | custom-call | tf_op jit(solution)/shard_map/jit(_cho_solve)/vmap()/triangular_solve | solution.py:40
  355.4 3.3 collective-permute-start.2
  358.7 2.8 collective-permute-done.2
  361.5 4.3 collective-permute-start.3
  365.9 5.0 collective-permute-done.3
  372.8 29.6 %all-gather.7.cloned.1.call-done = f32[4,1,2,128,256]{4,0,2,1,3:T(4,128)} async-done(((f32[4,1,2,32,256]{4,0,2,1,3:T(4,128)}), f32[4,1,2,128,256]{4,0,2,1,3:T(4,128)}) %all-gather.7.cloned.1.call-update) | async-done | bytes 1048592 | tf_op jit(solution)/shard_map/all_gather | solution.py:18
  403.9 3.3 collective-permute-start.4
  407.2 23.1 %collective-permute-done.4 = f32[4,2,4,32,256]{4,3,2,1,0:T(8,128)S(1)} collective-permute-done((f32[4,2,4,32,256]{4,3,2,1,0:T(8,128)S(1)}, f32[4,2,4,32,256]{4,3,2,1,0:T(8,128)S(1)}, u32[]{:S(2)}, u32[]{:S(2)}) %collective-permute-start.4) | collective-permute-done | bytes 1048608 | tf_op jit(solution)/shard_map/ppermute | solution.py:14
  432.8 4.3 collective-permute-start.5
  437.1 90.2 %collective-permute-done.5 = f32[4,2,256,256]{2,3,0,1:T(8,128)} collective-permute-done((f32[4,2,256,256]{2,3,0,1:T(8,128)}, f32[4,2,256,256]{2,3,0,1:T(8,128)}, u32[]{:S(2)}, u32[]{:S(2)}) %collective-permute-start.5) | collective-permute-done | bytes 2097184 | tf_op jit(solution)/shard_map/ppermute | solution.py:14
  536.9 47.1 %custom-call.23 = f32[4,128,128]{2,1,0:T(8,128)S(1)} custom-call(f32[4,128,128]{2,1,0:T(8,128)S(1)} %cholesky.201), custom_call_target="Cholesky" | custom-call | tf_op jit(solution)/shard_map/jit(cholesky)/cholesky | solution.py:39
  584.1 39.3 %custom-call.24 = f32[4,1,128,128]{2,3,1,0:T(8,128)S(1)} custom-call(f32[4,1,128,128]{3,2,1,0:T(8,128)S(1)} %select_bitcast_fusion), custom_call_target="InvertDiagBlocksLowerTriangular" | custom-call | tf_op jit(solution)/shard_map/jit(cholesky)/cholesky | solution.py:39
  626.4 46.9 %custom-call.25 = f32[4,128,128]{2,1,0:T(8,128)S(1)} custom-call(f32[4,128,128]{2,1,0:T(8,128)S(1)} %convolution_subtract_fusion.2), custom_call_target="Cholesky" | custom-call | tf_op jit(solution)/shard_map/jit(cholesky)/cholesky | solution.py:39
  673.9 4.1 while.5
  678.0 78.8 %custom-call.26 = f32[4,2,128,128]{2,3,1,0:T(8,128)S(1)} custom-call(f32[4,2,128,128]{3,2,1,0:T(8,128)S(1)} %bitcast.147), custom_call_target="InvertDiagBlocksLowerTriangular" | custom-call | tf_op jit(solution)/shard_map/jit(_cho_solve)/vmap()/triangular_solve | solution.py:40
  (97 shorter events, 59.9 us)
Async XLA Ops:
  6.5 59.2 %all-gather.5.cloned.1.call-start = ((), (), s32[]{:S(2)}) async-start(), calls=%async_computation | async-start | bytes 2621440 | tf_op jit(solution)/shard_map/all_gather | solution.py:18
  6.5 13.9 %collective-permute-start = (f32[4,2,64,256]{3,2,1,0:T(8,128)}, f32[4,2,64,256]{3,2,1,0:T(8,128)S(1)}, u32[]{:S(2)}, u32[]{:S(2)}) collective-permute-start(f32[4,2,64,256]{3,2,1,0:T(8,128)} %bitcast.149), channel_id=1, source_target_pairs={{0,1},{1,0},{2,3},{3,2},{4,5},{5,4},{6,7},{7,6},{8,9},{9,8},{10,11... | collective-permute-start | bytes 1572872 | tf_op jit(solution)/shard_map/ppermute | solution.py:14
  21.9 380.5 %all-gather.7.cloned.1.call-start = ((), (), s32[]{:S(2)}) async-start(), calls=%async_computation.1 | async-start | bytes 1310720 | tf_op jit(solution)/shard_map/all_gather | solution.py:18
  67.6 3.4 copy-start.2
  67.6 49.2 %collective-permute-start.1 = (f32[4,2,256,256]{2,3,0,1:T(8,128)S(1)}, f32[4,2,256,256]{2,3,0,1:T(8,128)}, u32[]{:S(2)}, u32[]{:S(2)}) collective-permute-start(f32[4,2,256,256]{2,3,0,1:T(8,128)S(1)} %bitcast.138), channel_id=1, source_target_pairs={{0,8},{8,0},{16,24},{24,16},{32,40},{40,32},{48,56},{56,48},{64,72... | collective-permute-start | bytes 6291464 | tf_op jit(solution)/shard_map/ppermute | solution.py:14
  119.6 2.0 copy-start.1
  125.8 1.0 copy-start.4
  347.1 2.9 copy-start.6
  351.7 2.3 copy-start.7
  355.4 6.1 collective-permute-start.2
  361.5 9.4 %collective-permute-start.3 = (f32[4,2,32,256]{3,2,1,0:T(8,128)S(1)}, f32[4,2,32,256]{3,2,1,0:T(8,128)S(1)}, u32[]{:S(2)}, u32[]{:S(2)}) collective-permute-start(f32[4,2,32,256]{3,2,1,0:T(8,128)S(1)} %maximum_select_fusion.4), channel_id=1, source_target_pairs={{0,1},{1,0},{2,3},{3,2},{4,5},{5,4},{6,7},{7,6},{8,9},{9,8},{10,11... | collective-permute-start | bytes 786440 | tf_op jit(solution)/shard_map/ppermute | solution.py:14
  371.0 0.8 copy-start.5
  403.9 26.4 %collective-permute-start.4 = (f32[4,2,4,32,256]{4,3,2,1,0:T(8,128)S(1)}, f32[4,2,4,32,256]{4,3,2,1,0:T(8,128)S(1)}, u32[]{:S(2)}, u32[]{:S(2)}) collective-permute-start(f32[4,2,4,32,256]{4,3,2,1,0:T(8,128)S(1)} %bitcast.139), channel_id=1, source_target_pairs={{0,8},{8,0},{16,24},{24,16},{32,40},{40,32},{48,56},{56,48},{64,72... | collective-permute-start | bytes 3145736 | tf_op jit(solution)/shard_map/ppermute | solution.py:14
  432.8 94.5 %collective-permute-start.5 = (f32[4,2,256,256]{2,3,0,1:T(8,128)}, f32[4,2,256,256]{2,3,0,1:T(8,128)}, u32[]{:S(2)}, u32[]{:S(2)}) collective-permute-start(f32[4,2,256,256]{2,3,0,1:T(8,128)} %copy.159), channel_id=1, source_target_pairs={{0,16},{16,0},{8,24},{24,8},{32,48},{48,32},{40,56},{56,40},{64,80... | collective-permute-start | bytes 6291464 | tf_op jit(solution)/shard_map/ppermute | solution.py:14
  530.0 1.6 copy-start
  535.9 1.0 copy-start.3
Sparse Core Ops, SparseCore 0:
  22.0 43.6 all-gather.4
  372.9 29.4 all-gather.6
where the time goes:
time: 774 us; the launch traced here: 771 us
  other arithmetic  439 us (57%)
  waiting for transfers between devices  248 us (32%)
  local copies, waits for them, and re-layouts  25.1 us (3%)
  starting transfers between devices  24 us (3%)
  matrix products  20.7 us (3%)
  between operations  14.2 us (2%)
    another operation x17, other arithmetic, merge(): factor = jnp.linalg.cholesky(system)  267 us
    ppermute x6, waiting for transfers between devices, from_partner(): return lax.ppermute(block, axis, route)  174 us
    another operation x6, other arithmetic, merge(): solved = jax.scipy.linalg.cho_solve((factor, True), target)  158 us
    all_gather x2, waiting for transfers between devices, gather_rows(): whole = lax.all_gather(stacked, 'tile', axis=2, tiled=True)  73.4 us
    ppermute x6, starting transfers between devices, from_partner(): return lax.ppermute(block, axis, route)  24 us
  transfers between devices with their start and end apart: 8, of which 8 were waited for; matrix products, arithmetic and copies ran while one was open for 0% of the time, Pallas kernels for 0%

commit v1 on v0

v1 whole, which is shorter than its diff:
```python
import jax
import jax.numpy as jnp
from jax import lax
from jax.experimental import pallas as pl
from jax.experimental.pallas import tpu as pltpu
from jax.sharding import PartitionSpec as P

HI = lax.Precision.HIGHEST

def dot(a, b, ca=1, cb=0):
    return lax.dot_general(a, b, (((ca,), (cb,)), ((), ())), precision=HI, preferred_element_type=jnp.float32)

def leaf(cols, sub):
    cols = list(cols)
    for k in range(8):
        piv = 1.0 / jnp.broadcast_to(cols[k][k:k+1, :], (8, 128))
        here = sub == k
        ck = cols[k]
        for c in range(8):
            if c == k:
                continue
            row = jnp.broadcast_to(cols[c][k:k+1, :], (8, 128)) * piv
            cols[c] = jnp.where(here, row, cols[c] - ck * row)
        cols[k] = jnp.where(here, piv, -ck * piv)
    return cols

def treesum(xs):
    while len(xs) > 1:
        xs = [xs[i] + xs[i+1] if i + 1 < len(xs) else xs[i] for i in range(0, len(xs), 2)]
    return xs[0]

def apply8(cols, y):
    return treesum([cols[j] * jnp.broadcast_to(y[j:j+1, :], (8, 128)) for j in range(8)])

def eliminate(mats):
    sub = lax.broadcasted_iota(jnp.int32, (8, 128), 0)
    lane = lax.broadcasted_iota(jnp.int32, (8, 128), 1)
    mats = [list(m) for m in mats]
    es = [[] for _ in mats]
    des = [[] for _ in mats]
    for k in range(16):
        lo = 8 * k
        inblk = (lane >= lo) & (lane < lo + 8)
        eye = jnp.where(lane == sub + lo, 1.0, 0.0).astype(jnp.float32)
        for n, m in enumerate(mats):
            r = m[k]
            cols = leaf([jnp.broadcast_to(r[:, lo+c:lo+c+1], (8, 128)) for c in range(8)], sub)
            rm = jnp.where(inblk, eye, r)
            y = apply8(cols, rm)
            es[n].append(jnp.where(lane < lo + 8, rm, 0.0))
            des[n].append(jnp.where(lane < lo + 8, y, 0.0))
            ys = [jnp.broadcast_to(y[j:j+1, :], (8, 128)) for j in range(8)]
            for i in range(k + 1, 16):
                a = m[i]
                upd = treesum([jnp.broadcast_to(a[:, lo+j:lo+j+1], (8, 128)) * ys[j] for j in range(8)])
                m[i] = jnp.where(inblk, 0.0, a) - upd
    return es, des

def factor(mat_refs, fac_refs):
    es, des = eliminate([[m[8*i:8*i+8, :] for i in range(16)] for m in mat_refs])
    for f, e, d in zip(fac_refs, es, des):
        for i in range(16):
            f[8*i:8*i+8, :] = e[i]
            f[128+8*i:128+8*i+8, :] = d[i]

def solve(aug, fac, vs, ys, width):
    factor([a.at[0:128, 0:128] for a in aug], fac)
    for a, f, v, y in zip(aug, fac, vs, ys):
        vy = dot(f[...], a[0:128, 128:])
        v[0:128, :] = vy[0:128, 128:]
        y[0:128, :] = vy[128:, 128:]
        a[128:256, 128:] = a[128:256, 128:] - dot(vy[0:128, 0:128], vy[128:, :], 0, 0)
    factor([a.at[128:256, 128:256] for a in aug], fac)
    for a, f, v, y in zip(aug, fac, vs, ys):
        vy = dot(f[...], a[128:256, 256:])
        v[128:256, :] = vy[0:128, :]
        y[128:256, :] = vy[128:, :]

def kernel(g_ref, d_ref, o_ref, a0, a1, a2, v0, v1, v2, y0, y1, y2, f0, f1):
    tile = lax.axis_index("tile")
    col = lax.axis_index("col")
    for p, a in enumerate((a0, a1)):
        a[:, 0:256] = g_ref[0, p] + g_ref[1, p]
        a[:, 256:512] = g_ref[0, 2 + p]
        a[:, 512:768] = g_ref[1, 2 + p]
    solve((a0, a1), (f0, f1), (v0, v1), (y0, y1), 512)
    p0 = dot(v0[:, 256:512], y0[...], 0, 0)
    p1 = dot(v1[:, 0:256], y1[...], 0, 0)
    a2[:, 0:256] = g_ref[0, 4] + g_ref[1, 4] - p0[:, 256:512] - p1[:, 0:256]
    a2[:, 256:512] = -p0[:, 0:256]
    a2[:, 512:768] = -p1[:, 256:512]
    solve((a2,), (f0,), (v2,), (y2,), 512)
    start = pl.multiple_of(tile // 2 * 128, 128)
    half = tile % 2
    cols = pl.multiple_of(col * 256, 256)
    a0[:, 0:128] = v2[:, pl.ds(start, 128)]
    a0[:, 128:256] = v2[:, pl.ds(start + 256, 128)]
    a0[:, 256:512] = y2[:, pl.ds(cols, 256)]
    a1[:, 0:128] = jnp.where(col == 0, v0[:, pl.ds(start, 128)], v1[:, pl.ds(start + 256, 128)])
    a1[:, 256:512] = jnp.where(col == 0, y0[:, 0:256], y1[:, 256:512])
    a2[:, 0:256] = dot(a0[:, 0:256], a0[:, 256:512], 0, 0)
    a2[0:128, 256:512] = dot(a1[:, 0:128], a1[:, 256:512], 0, 0)
    row = pl.multiple_of(half * 64, 64)
    own = d_ref[...] - a2[pl.ds(row, 64), 256:512]
    o_ref[0:64, :] = jnp.where(col == 0, own, 0.0) - a2[pl.ds(row, 64), 0:256]
    o_ref[64:128, :] = jnp.where(col == 1, own, 0.0) - a2[pl.ds(128 + row, 64), 0:256]


def call(g, d):
    V = pltpu.VMEM
    f = jnp.float32
    return pl.pallas_call(
        kernel,
        out_shape=jax.ShapeDtypeStruct((128, 256), f),
        scratch_shapes=[V((256, 768), f)] * 3 + [V((256, 512), f)] * 6 + [V((256, 128), f)] * 2,
        compiler_params=pltpu.CompilerParams(vmem_limit_bytes=40 << 20),
    )(g, d)


def per_device(box_operators):
    x = box_operators[:, 0]
    boxes = lax.axis_size("box")
    groups = [[4 * q + b for b in range(4)] for q in range(boxes // 4)]
    parts = lax.all_to_all(x, "box", 0, 0, axis_index_groups=groups, tiled=True)
    c0 = jnp.stack([parts[1, 0], parts[3, 0], parts[0, 1], parts[2, 1], parts[2, 0]])
    c1 = jnp.stack([parts[0, 1], parts[2, 1], parts[1, 0], parts[3, 0], parts[1, 1]])
    col = lax.axis_index("col")
    mine = jnp.where(col == 0, c0, c1)
    own = jnp.where(col == 0, parts[0, 0], parts[3, 1])
    g = lax.all_gather(mine, "tile", axis=1, tiled=True)
    g = lax.all_gather(g, "col", axis=0)
    out = call(g, own)
    out = out.reshape(4, 32, 256)
    out = lax.all_to_all(out, "box", 0, 0, axis_index_groups=groups, tiled=True)
    return out[:, None]


def solution(mesh):
    return jax.shard_map(
        per_device,
        mesh=mesh,
        in_specs=(P(None, "box", None, "tile", "col"),),
        out_specs=P(None, "box", "tile", "col"),
        check_vma=False,
    )
```

time: 774 us -> 158 us (0.20)
  other arithmetic: 439 us -> 0.77 us
  waiting for transfers between devices: 248 us -> 96.3 us
  Pallas kernels: 0 us -> 27 us
  local copies, waits for them, and re-layouts: 25.1 us -> 2.45 us
  matrix products: 20.7 us -> 0 us
  starting transfers between devices: 24 us -> 7.85 us
  blocking collectives: 0 us -> 9.41 us
    another operation x24 -> x0, other arithmetic: 426 us -> none  [the longest x17 267 us: merge(): factor = jnp.linalg.cholesky(system)]
    ppermute x6 -> x0, waiting for transfers between devices: 174 us -> none  [from_partner(): return lax.ppermute(block, axis, route)]
    pallas_call x0 -> x1, Pallas kernels: none -> 27 us  [call(): pl.pallas_call(kernel, out_shape=jax.ShapeDtypeStruct((128, 256), f), scr...]
    ppermute x6 -> x0, starting transfers between devices: 24 us -> none  [from_partner(): return lax.ppermute(block, axis, route)]
    another operation x16 -> x0, matrix products: 17.5 us -> none  [the longest x12 11.5 us: merge(): solved = jax.scipy.linalg.cho_solve((factor, True), target)]
    all_to_all x0 -> x1, waiting for transfers between devices: none -> 13.1 us  [per_device(): parts = lax.all_to_all(x, 'box', 0, 0, axis_index_groups=groups, tiled=True)]
    all_gather x2, waiting for transfers between devices: 73.4 us -> 83.1 us  [the longest x1 51 us: per_device(): g = lax.all_gather(g, 'col', axis=0)]
    all_to_all x0 -> x1, blocking collectives: none -> 9.41 us  [per_device(): out = lax.all_to_all(out, 'box', 0, 0, axis_index_groups=groups, tiled=True)]
  transfers between devices with their start and end apart: 8 -> 3, of which waited for: 8 -> 3; matrix products, arithmetic and copies ran while one was open for 0% -> 0% of each run, Pallas kernels for 0% -> 0%
where the time goes in v1:
time: 158 us; the launch traced here: 157 us
  waiting for transfers between devices  96.3 us (61%)
  Pallas kernels  27 us (17%)
  between operations  13.5 us (9%)
  blocking collectives  9.41 us (6%)
  starting transfers between devices  7.85 us (5%)
  local copies, waits for them, and re-layouts  2.45 us (2%)
    all_gather x1, waiting for transfers between devices, per_device(): g = lax.all_gather(g, 'col', axis=0)  51 us
    all_gather x1, waiting for transfers between devices, per_device(): g = lax.all_gather(mine, 'tile', axis=1, tiled=True)  32.1 us
    pallas_call x1, Pallas kernels, call(): pl.pallas_call(kernel, out_shape=jax.ShapeDtypeStruct((128, 256), f), scr...  27 us
    all_to_all x1, waiting for transfers between devices, per_device(): parts = lax.all_to_all(x, 'box', 0, 0, axis_index_groups=groups, tiled=True)  13.1 us
    all_to_all x1, blocking collectives, per_device(): out = lax.all_to_all(out, 'box', 0, 0, axis_index_groups=groups, tiled=True)  9.41 us
    all_to_all x1, starting transfers between devices, per_device(): parts = lax.all_to_all(x, 'box', 0, 0, axis_index_groups=groups, tiled=True)  7.81 us
  transfers between devices with their start and end apart: 3, of which 3 were waited for; matrix products, arithmetic and copies ran while one was open for 0% of the time, Pallas kernels for 0%

profile of v1, /device:TPU:1, one launch (start us, length us, event | category | flops | bytes accessed | tf_op | source)
XLA Modules:
  0.0 157.2 jit_solution(15196545877178392876)
XLA Ops:
  6.5 7.8 %all-to-all-start = ((f32[4,2,64,256]{3,2,1,0:T(8,128)}), f32[4,2,64,256]{3,2,1,0:T(8,128)S(1)}, u32[]{:S(2)}, u32[]{:S(2)}) async-start(f32[4,2,64,256]{3,2,1,0:T(8,128)} %bitcast.40), calls=%async_computation | async-start | bytes 1048576 | tf_op jit(solution)/shard_map/all_to_all | solution.py:124
  14.3 0.0 all-gather.4.cloned.1.call-start
  14.3 13.1 %all-to-all-done = f32[4,2,64,256]{3,2,1,0:T(8,128)S(1)} async-done(((f32[4,2,64,256]{3,2,1,0:T(8,128)}), f32[4,2,64,256]{3,2,1,0:T(8,128)S(1)}, u32[]{:S(2)}, u32[]{:S(2)}) %all-to-all-start) | async-done | bytes 524320 | tf_op jit(solution)/shard_map/all_to_all | solution.py:124
  27.6 0.8 broadcast_select_fusion
  28.3 0.0 all-gather.4.cloned.1.call-update
  28.3 0.0 all-gather.6.cloned.1.call-start
  28.4 32.1 %all-gather.4.cloned.1.call-done = f32[5,256,256]{2,1,0:T(8,128)} async-done(((f32[5,64,256]{2,1,0:T(8,128)}), f32[5,256,256]{2,1,0:T(8,128)}) %all-gather.4.cloned.1.call-update) | async-done | bytes 1310736 | tf_op jit(solution)/shard_map/all_gather | solution.py:130
  60.5 0.0 all-gather.6.cloned.1.call-update
  60.5 51.0 %all-gather.6.cloned.1.call-done = f32[10,256,256]{2,1,0:T(8,128)} async-done(((f32[5,256,256]{2,1,0:T(8,128)}), f32[10,256,256]{2,1,0:T(8,128)}) %all-gather.6.cloned.1.call-update) | async-done | bytes 2621456 | tf_op jit(solution)/shard_map/all_gather | solution.py:131
  111.6 0.0 copy-start
  111.6 1.7 %copy-done = f32[10,256,256]{2,1,0:T(8,128)S(1)} copy-done((f32[10,256,256]{2,1,0:T(8,128)S(1)}, f32[10,256,256]{2,1,0:T(8,128)}, u32[]{:S(2)}) %copy-start) | copy-done | bytes 2621464
  113.3 27.0 %shard_map.17 = f32[128,256]{1,0:T(8,128)S(1)} custom-call(f32[2,5,256,256]{3,2,1,0:T(8,128)S(1)} %bitcast.38, f32[64,256]{1,0:T(8,128)S(1)} %fusion.d_ref), custom_call_target="tpu_custom_call" | custom-call | tf_op jit(solution)/shard_map/pallas_call | solution.py:112
  140.3 9.4 %all_to_all.10 = f32[4,32,256]{2,1,0:T(8,128)S(1)} all-to-all(f32[4,32,256]{2,1,0:T(8,128)S(1)} %bitcast.39), channel_id=1, replica_groups={{0,8,16,24},{32,40,48,56},{64,72,80,88},{96,104,112,120},{128,136,144,1..., dimensions={0} | all-to-all | bytes 262144 | tf_op jit(solution)/shard_map/all_to_all | solution.py:134
  149.7 0.7 copy.11
  (6 shorter events, 0.1 us)
Async XLA Ops:
  6.5 20.9 %all-to-all-start = ((f32[4,2,64,256]{3,2,1,0:T(8,128)}), f32[4,2,64,256]{3,2,1,0:T(8,128)S(1)}, u32[]{:S(2)}, u32[]{:S(2)}) async-start(f32[4,2,64,256]{3,2,1,0:T(8,128)} %bitcast.40), calls=%async_computation | async-start | bytes 1048576 | tf_op jit(solution)/shard_map/all_to_all | solution.py:124
  14.3 46.1 %all-gather.4.cloned.1.call-start = ((), (), s32[]{:S(2)}) async-start(), calls=%async_computation.2 | async-start | bytes 1638400 | tf_op jit(solution)/shard_map/all_gather | solution.py:130
  28.3 83.2 %all-gather.6.cloned.1.call-start = ((), (), s32[]{:S(2)}) async-start(), calls=%async_computation.3 | async-start | bytes 3932160 | tf_op jit(solution)/shard_map/all_gather | solution.py:131
  111.6 1.7 %copy-start = (f32[10,256,256]{2,1,0:T(8,128)S(1)}, f32[10,256,256]{2,1,0:T(8,128)}, u32[]{:S(2)}) copy-start(f32[10,256,256]{2,1,0:T(8,128)} %all-gather.6.cloned.1.call-done) | copy-start | bytes 7864324
Sparse Core Ops, SparseCore 0:
  28.5 31.9 all-gather.3
  62.6 48.9 all-gather.5

commit v2 on v1

--- a/solution.py
+++ b/solution.py
@@ -63,35 +63,171 @@
             f[8*i:8*i+8, :] = e[i]
             f[128+8*i:128+8*i+8, :] = d[i]
 
-def solve(aug, fac, vs, ys, width):
-    factor([a.at[0:128, 0:128] for a in aug], fac)
-    for a, f, v, y in zip(aug, fac, vs, ys):
-        vy = dot(f[...], a[0:128, 128:])
-        v[0:128, :] = vy[0:128, 128:]
-        y[0:128, :] = vy[128:, 128:]
-        a[128:256, 128:] = a[128:256, 128:] - dot(vy[0:128, 0:128], vy[128:, :], 0, 0)
-    factor([a.at[128:256, 128:256] for a in aug], fac)
-    for a, f, v, y in zip(aug, fac, vs, ys):
-        vy = dot(f[...], a[128:256, 256:])
-        v[128:256, :] = vy[0:128, :]
-        y[128:256, :] = vy[128:, :]
-
-def kernel(g_ref, d_ref, o_ref, a0, a1, a2, v0, v1, v2, y0, y1, y2, f0, f1):
+def solve(a, fac, v, y):
+    factor([a.at[0:128, 0:128]], [fac])
+    vy = dot(fac[...], a[0:128, 128:])
+    v[0:128, :] = vy[0:128, 128:]
+    y[0:128, :] = vy[128:, 128:]
+    a[128:256, 128:] = a[128:256, 128:] - dot(vy[0:128, 0:128], vy[128:, :], 0, 0)
+    factor([a.at[128:256, 128:256]], [fac])
+    vy = dot(fac[...], a[128:256, 256:])
+    v[128:256, :] = vy[0:128, :]
+    y[128:256, :] = vy[128:, :]
+
+
+MESH = pl.DeviceIdType.MESH
+SLOTS = 5
+
+
+def kernel(x_ref, out_ref, g, ob, a0, a1, a2, v0, v1, v2, y0, y1, y2, f0, f1, f2, f3,
+           send1, recv1, send2, recv2, sendo, recvo):
+    box = lax.axis_index("box")
     tile = lax.axis_index("tile")
     col = lax.axis_index("col")
+    b = box % 4
+    quad = box - b
+    core = tile % 2
+    x = 2 * col + tile // 2
+    ring = [((x + d) % 4 // 2, (x + d) % 4 % 2 * 2 + core) for d in range(4)]
+    right = {"col": ring[1][0], "tile": ring[1][1]}
+    left = {"col": ring[3][0], "tile": ring[3][1]}
+    across = {"col": ring[2][0], "tile": ring[2][1]}
+    sib = {"tile": tile + 1 - 2 * core}
+    line = [{"box": quad + (b + d) % 4} for d in range(4)]
+
+    barrier = pltpu.get_barrier_semaphore()
+    for dev in (right, left, sib, line[1], line[2], line[3]):
+        pl.semaphore_signal(barrier, inc=1, device_id=dev, device_id_type=MESH)
+    pl.semaphore_wait(barrier, 6)
+
+    def piece(slot, d, lo=0, n=64):
+        c, t = ring[d]
+        return g.at[c, slot, pl.ds(pl.multiple_of(t * 64 + lo, 32), n), :]
+
+    def remote(src, dst, s, r, dev):
+        return pltpu.make_async_remote_copy(src_ref=src, dst_ref=dst, send_sem=s, recv_sem=r,
+                                            device_id=dev, device_id_type=MESH)
+
+    def first(kind, face, slot):
+        away = [remote(x_ref.at[(b + d) % 4, face], piece(slot, 0), send1.at[kind, d - 1], recv1.at[slot], line[d])
+                for d in (1, 2, 3)]
+        home = pltpu.make_async_copy(x_ref.at[b, face], piece(slot, 0), recv1.at[slot])
+        return away, home
+
+    is_s = col != b % 2
+    own_slot = jnp.where((b == 1) | (b == 2), 4, 5)
+
+    @pl.when(is_s)
+    def _():
+        away, home = first(0, col, b // 2)
+        home.start()
+        for c in away:
+            c.start()
+
+    @pl.when(jnp.logical_not(is_s))
+    def _():
+        for kind, face, slot in ((0, 1 - col, 2 + b // 2), (1, col, own_slot)):
+            away, home = first(kind, face, slot)
+            home.start()
+            for c in away:
+                c.start()
+
+    def wait1(slot):
+        pltpu.make_async_copy(piece(slot, 0), piece(slot, 0), recv1.at[slot]).wait()
+
+    TO_R, TO_L, TO_S, FW_R, FW_L, SIB_L, SIB_R, SIB_A, SIB_B = range(9)
+    via = {0: ((0, 64), None), 1: (None, (0, 64)), 2: ((0, 64), None), 3: (None, (0, 64)), 4: ((0, 32), (32, 32))}
+    started = []
+
+    def go(kind, slot, src_d, lo, n, row, dev):
+        p = piece(slot, src_d, lo, n)
+        c = remote(p, p, send2.at[kind, slot], recv2.at[row, slot], dev)
+        c.start()
+        started.append(c)
+
+    def arrived(slot, d, lo, n, row):
+        p = piece(slot, d, lo, n)
+        pltpu.make_async_copy(p, p, recv2.at[row, slot]).wait()
+
+    def s2_start(slot):
+        wait1(slot)
+        go(TO_R, slot, 0, 0, 64, 0, right)
+        go(TO_L, slot, 0, 0, 64, 1, left)
+        go(TO_S, slot, 0, 0, 64, 4, sib)
+
+    def s2_fwd(slot):
+        by_r, by_l = via[slot]
+        arrived(slot, 3, 0, 64, 0)
+        if by_r:
+            go(FW_R, slot, 3, by_r[0], by_r[1], 2, right)
+        go(SIB_L, slot, 3, 0, 64, 5, sib)
+        arrived(slot, 1, 0, 64, 1)
+        if by_l:
+            go(FW_L, slot, 1, by_l[0], by_l[1], 3, left)
+        go(SIB_R, slot, 1, 0, 64, 6, sib)
+
+    def s2_last(slot):
+        for part, row, kind, to in zip(via[slot], (2, 3), (SIB_A, SIB_B), (7, 8)):
+            if part:
+                arrived(slot, 2, part[0], part[1], row)
+                go(kind, slot, 2, part[0], part[1], to, sib)
+
+    def s2_done(slot):
+        def other(d, lo, n, row):
+            c, t = ring[d]
+            p = g.at[c, slot, pl.ds(pl.multiple_of((t + 1 - 2 * core) * 64 + lo, 32), n), :]
+            pltpu.make_async_copy(p, p, recv2.at[row, slot]).wait()
+        other(0, 0, 64, 4)
+        other(3, 0, 64, 5)
+        other(1, 0, 64, 6)
+        for part, row in zip(via[slot], (7, 8)):
+            if part:
+                other(2, part[0], part[1], row)
+
+    for s in (0, 1):
+        s2_start(s)
+    for s in (0, 1):
+        s2_fwd(s)
+    for s in (2, 3, 4):
+        s2_start(s)
+    for s in (0, 1):
+        s2_last(s)
+    for s in (0, 1):
+        s2_done(s)
+
     for p, a in enumerate((a0, a1)):
-        a[:, 0:256] = g_ref[0, p] + g_ref[1, p]
-        a[:, 256:512] = g_ref[0, 2 + p]
-        a[:, 512:768] = g_ref[1, 2 + p]
-    solve((a0, a1), (f0, f1), (v0, v1), (y0, y1), 512)
+        a[:, 0:256] = g[0, p] + g[1, p]
+    factor([a.at[0:128, 0:128] for a in (a0, a1)], [f0, f1])
+    for s in (2, 3, 4):
+        s2_fwd(s)
+    for a, f in ((a0, f0), (a1, f1)):
+        vy = dot(f[...], a[0:128, 128:256])
+        a[0:128, 0:128] = vy[0:128]
+        a[128:256, 128:256] = a[128:256, 128:256] - dot(vy[0:128], vy[128:], 0, 0)
+    factor([a.at[128:256, 128:256] for a in (a0, a1)], [f2, f3])
+    for s in (2, 3, 4):
+        s2_last(s)
+    for s in (2, 3, 4):
+        s2_done(s)
+    for p, a in enumerate((a0, a1)):
+        a[:, 256:512] = g[0, 2 + p]
+        a[:, 512:768] = g[1, 2 + p]
+    for a, f, h, v, y in ((a0, f0, f2, v0, y0), (a1, f1, f3, v1, y1)):
+        vy = dot(f[...], a[0:128, 256:])
+        v[0:128, :] = vy[0:128]
+        y[0:128, :] = vy[128:]
+        vy = dot(h[...], a[128:256, 256:] - dot(a[0:128, 0:128], vy[128:], 0, 0))
+        v[128:256, :] = vy[0:128]
+        y[128:256, :] = vy[128:]
+
     p0 = dot(v0[:, 256:512], y0[...], 0, 0)
     p1 = dot(v1[:, 0:256], y1[...], 0, 0)
-    a2[:, 0:256] = g_ref[0, 4] + g_ref[1, 4] - p0[:, 256:512] - p1[:, 0:256]
+    a2[:, 0:256] = g[0, 4] + g[1, 4] - p0[:, 256:512] - p1[:, 0:256]
     a2[:, 256:512] = -p0[:, 0:256]
     a2[:, 512:768] = -p1[:, 256:512]
-    solve((a2,), (f0,), (v2,), (y2,), 512)
+    solve(a2, f0, v2, y2)
+
     start = pl.multiple_of(tile // 2 * 128, 128)
-    half = tile % 2
     cols = pl.multiple_of(col * 256, 256)
     a0[:, 0:128] = v2[:, pl.ds(start, 128)]
     a0[:, 128:256] = v2[:, pl.ds(start + 256, 128)]
@@ -100,38 +236,55 @@
     a1[:, 256:512] = jnp.where(col == 0, y0[:, 0:256], y1[:, 256:512])
     a2[:, 0:256] = dot(a0[:, 0:256], a0[:, 256:512], 0, 0)
     a2[0:128, 256:512] = dot(a1[:, 0:128], a1[:, 256:512], 0, 0)
-    row = pl.multiple_of(half * 64, 64)
-    own = d_ref[...] - a2[pl.ds(row, 64), 256:512]
-    o_ref[0:64, :] = jnp.where(col == 0, own, 0.0) - a2[pl.ds(row, 64), 0:256]
-    o_ref[64:128, :] = jnp.where(col == 1, own, 0.0) - a2[pl.ds(128 + row, 64), 0:256]
-
-
-def call(g, d):
+    row = pl.multiple_of(core * 64, 64)
+    wait1(5)
+    own = g[col, 5, pl.ds(pl.multiple_of(tile * 64, 64), 64), :] - a2[pl.ds(row, 64), 256:512]
+    ob[0:64, :] = jnp.where(col == 0, own, 0.0) - a2[pl.ds(row, 64), 0:256]
+    ob[64:128, :] = jnp.where(col == 1, own, 0.0) - a2[pl.ds(128 + row, 64), 0:256]
+
+    def result(to):
+        return ob.at[pl.ds(pl.multiple_of(to * 32, 32), 32), :]
+
+    outs = [remote(result((b + d) % 4), out_ref.at[b], sendo.at[d - 1], recvo.at[d - 1], line[d]) for d in (1, 2, 3)]
+    for c in outs:
+        c.start()
+    home = pltpu.make_async_copy(result(b), out_ref.at[b], recvo.at[3])
+    home.start()
+    for c in outs:
+        c.wait_send()
+    for d in (1, 2, 3):
+        p = out_ref.at[(b + 4 - d) % 4]
+        pltpu.make_async_copy(p, p, recvo.at[d - 1]).wait()
+    home.wait()
+    for c in started:
+        c.wait_send()
+
+    @pl.when(is_s)
+    def _():
+        for c in first(0, col, b // 2)[0]:
+            c.wait_send()
+
+    @pl.when(jnp.logical_not(is_s))
+    def _():
+        for kind, face, slot in ((0, 1 - col, 2 + b // 2), (1, col, own_slot)):
+            for c in first(kind, face, slot)[0]:
+                c.wait_send()
+
+
+def per_device(box_operators):
     V = pltpu.VMEM
     f = jnp.float32
-    return pl.pallas_call(
+    dma = pltpu.SemaphoreType.DMA
+    out = pl.pallas_call(
         kernel,
-        out_shape=jax.ShapeDtypeStruct((128, 256), f),
-        scratch_shapes=[V((256, 768), f)] * 3 + [V((256, 512), f)] * 6 + [V((256, 128), f)] * 2,
-        compiler_params=pltpu.CompilerParams(vmem_limit_bytes=40 << 20),
-    )(g, d)
-
-
-def per_device(box_operators):
-    x = box_operators[:, 0]
-    boxes = lax.axis_size("box")
-    groups = [[4 * q + b for b in range(4)] for q in range(boxes // 4)]
-    parts = lax.all_to_all(x, "box", 0, 0, axis_index_groups=groups, tiled=True)
-    c0 = jnp.stack([parts[1, 0], parts[3, 0], parts[0, 1], parts[2, 1], parts[2, 0]])
-    c1 = jnp.stack([parts[0, 1], parts[2, 1], parts[1, 0], parts[3, 0], parts[1, 1]])
-    col = lax.axis_index("col")
-    mine = jnp.where(col == 0, c0, c1)
-    own = jnp.where(col == 0, parts[0, 0], parts[3, 1])
-    g = lax.all_gather(mine, "tile", axis=1, tiled=True)
-    g = lax.all_gather(g, "col", axis=0)
-    out = call(g, own)
-    out = out.reshape(4, 32, 256)
-    out = lax.all_to_all(out, "box", 0, 0, axis_index_groups=groups, tiled=True)
+        out_shape=jax.ShapeDtypeStruct((4, 32, 256), f),
+        in_specs=[pl.BlockSpec(memory_space=pl.ANY)],
+        out_specs=pl.BlockSpec(memory_space=pl.ANY),
+        scratch_shapes=[V((2, 6, 256, 256), f), V((128, 256), f)] + [V((256, 768), f)] * 3 + [V((256, 512), f)] * 6
+        + [V((256, 128), f)] * 4
+        + [dma((2, 3)), dma((6,)), dma((9, SLOTS)), dma((9, SLOTS)), dma((3,)), dma((4,))],
+        compiler_params=pltpu.CompilerParams(vmem_limit_bytes=40 << 20, collective_id=0, has_side_effects=True),
+    )(box_operators[:, 0])
     return out[:, None]
 
 

time: 158 us -> 61.2 us (0.39)
  waiting for transfers between devices: 96.3 us -> 0 us
  Pallas kernels: 27 us -> 59.1 us
  between operations: 13.5 us -> 0.01 us
  blocking collectives: 9.41 us -> 0 us
  starting transfers between devices: 7.85 us -> 0 us
    all_gather x2 -> x0, waiting for transfers between devices: 83.1 us -> none  [the longest x1 51 us: per_device(): g = lax.all_gather(g, 'col', axis=0)]
    pallas_call x1, Pallas kernels: 27 us -> 59.1 us  [per_device(): pl.pallas_call(kernel, out_shape=jax.ShapeDtypeStruct((4, 32, 256), f), i...]
    all_to_all x1 -> x0, waiting for transfers between devices: 13.1 us -> none  [per_device(): parts = lax.all_to_all(x, 'box', 0, 0, axis_index_groups=groups, tiled=True)]
    all_to_all x1 -> x0, blocking collectives: 9.41 us -> none  [per_device(): out = lax.all_to_all(out, 'box', 0, 0, axis_index_groups=groups, tiled=True)]
    all_to_all x1 -> x0, starting transfers between devices: 7.81 us -> none  [per_device(): parts = lax.all_to_all(x, 'box', 0, 0, axis_index_groups=groups, tiled=True)]
  transfers between devices with their start and end apart: 3 -> 0, of which waited for: 3 -> 0; matrix products, arithmetic and copies ran while one was open for 0% -> 0% of each run, Pallas kernels for 0% -> 0%
where the time goes in v2:
time: 61.2 us; the launch traced here: 60.8 us
  Pallas kernels  59.1 us (97%)
  local copies, waits for them, and re-layouts  1.7 us (3%)
    pallas_call x1, Pallas kernels, per_device(): pl.pallas_call(kernel, out_shape=jax.ShapeDtypeStruct((4, 32, 256), f), i...  59.1 us
    unnamed x3, local copies, waits for them, and re-layouts  1.7 us

profile of v2, /device:TPU:1, one launch (start us, length us, event | category | flops | bytes accessed | tf_op | source)
XLA Modules:
  0.0 60.8 jit_solution(9254359862937401511)
XLA Ops:
  0.0 0.0 copy-start
  0.0 1.0 %copy-done = f32[4,1,2,64,256]{4,3,2,1,0:T(8,128)S(1)} copy-done((f32[4,1,2,64,256]{4,3,2,1,0:T(8,128)S(1)}, f32[4,1,2,64,256]{4,3,2,1,0:T(8,128)}, u32[]{:S(2)}) %copy-start) | copy-done | bytes 524312
  1.0 59.1 %shard_map.17 = f32[4,32,256]{2,1,0:T(8,128)S(1)} custom-call(f32[4,2,64,256]{3,2,1,0:T(8,128)S(1)} %bitcast.4), custom_call_target="tpu_custom_call" | custom-call | tf_op jit(solution)/shard_map/pallas_call | solution.py:278
  60.1 0.7 %copy.4 = f32[4,1,32,256]{3,2,1,0:T(8,128)} copy(f32[4,1,32,256]{3,2,1,0:T(8,128)S(1)} %bitcast.5) | data formatting | bytes 262144
Async XLA Ops:
  0.0 1.0 %copy-start = (f32[4,1,2,64,256]{4,3,2,1,0:T(8,128)S(1)}, f32[4,1,2,64,256]{4,3,2,1,0:T(8,128)}, u32[]{:S(2)}) copy-start(f32[4,1,2,64,256]{4,3,2,1,0:T(8,128)} %param.1) | copy-start | bytes 1572868

commit v3 on v1

v3 whole, which is shorter than its diff:
```python
import jax
import jax.numpy as jnp
from jax import lax
from jax.experimental import pallas as pl
from jax.experimental.pallas import tpu as pltpu
from jax.sharding import PartitionSpec as P

HI = lax.Precision.HIGHEST

def dot(a, b, ca=1, cb=0):
    return lax.dot_general(a, b, (((ca,), (cb,)), ((), ())), precision=HI, preferred_element_type=jnp.float32)

def leaf(cols, sub):
    cols = list(cols)
    for k in range(8):
        piv = 1.0 / jnp.broadcast_to(cols[k][k:k+1, :], (8, 128))
        here = sub == k
        ck = cols[k]
        for c in range(8):
            if c == k:
                continue
            row = jnp.broadcast_to(cols[c][k:k+1, :], (8, 128)) * piv
            cols[c] = jnp.where(here, row, cols[c] - ck * row)
        cols[k] = jnp.where(here, piv, -ck * piv)
    return cols

def treesum(xs):
    while len(xs) > 1:
        xs = [xs[i] + xs[i+1] if i + 1 < len(xs) else xs[i] for i in range(0, len(xs), 2)]
    return xs[0]

def apply8(cols, y):
    return treesum([cols[j] * jnp.broadcast_to(y[j:j+1, :], (8, 128)) for j in range(8)])

def eliminate(mats, hook=None):
    sub = lax.broadcasted_iota(jnp.int32, (8, 128), 0)
    lane = lax.broadcasted_iota(jnp.int32, (8, 128), 1)
    mats = [list(m) for m in mats]
    es = [[] for _ in mats]
    des = [[] for _ in mats]
    for k in range(16):
        if hook is not None:
            hook(k)
        lo = 8 * k
        inblk = (lane >= lo) & (lane < lo + 8)
        eye = jnp.where(lane == sub + lo, 1.0, 0.0).astype(jnp.float32)
        for n, m in enumerate(mats):
            r = m[k]
            cols = leaf([jnp.broadcast_to(r[:, lo+c:lo+c+1], (8, 128)) for c in range(8)], sub)
            rm = jnp.where(inblk, eye, r)
            y = apply8(cols, rm)
            es[n].append(jnp.where(lane < lo + 8, rm, 0.0))
            des[n].append(jnp.where(lane < lo + 8, y, 0.0))
            ys = [jnp.broadcast_to(y[j:j+1, :], (8, 128)) for j in range(8)]
            for i in range(k + 1, 16):
                a = m[i]
                upd = treesum([jnp.broadcast_to(a[:, lo+j:lo+j+1], (8, 128)) * ys[j] for j in range(8)])
                m[i] = jnp.where(inblk, 0.0, a) - upd
    return es, des

def factor(mat_refs, fac_refs, hook=None):
    es, des = eliminate([[m[8*i:8*i+8, :] for i in range(16)] for m in mat_refs], hook)
    for f, e, d in zip(fac_refs, es, des):
        for i in range(16):
            f[8*i:8*i+8, :] = e[i]
            f[128+8*i:128+8*i+8, :] = d[i]

def solve(a, fac, v, y):
    factor([a.at[0:128, 0:128]], [fac])
    vy = dot(fac[...], a[0:128, 128:])
    v[0:128, :] = vy[0:128, 128:]
    y[0:128, :] = vy[128:, 128:]
    a[128:256, 128:] = a[128:256, 128:] - dot(vy[0:128, 0:128], vy[128:, :], 0, 0)
    factor([a.at[128:256, 128:256]], [fac])
    vy = dot(fac[...], a[128:256, 256:])
    v[128:256, :] = vy[0:128, :]
    y[128:256, :] = vy[128:, :]


MESH = pl.DeviceIdType.MESH

def kernel(x_ref, out_ref, g, ob, a0, a1, a2, v0, v1, v2, y0, y1, y2, f0, f1, f2, f3,
           send1, recv1, send2, recv2, sendo, recvo):
    box = lax.axis_index("box")
    tile = lax.axis_index("tile")
    col = lax.axis_index("col")
    b = box % 4
    quad = box - b
    core = tile % 2
    x = 2 * col + tile // 2

    def at(dz, dx):
        xx = (x + dx) % 4
        return {"box": quad + (b + dz) % 4, "col": xx // 2, "tile": xx % 2 * 2 + core}

    sib = {"tile": tile + 1 - 2 * core}

    barrier = pltpu.get_barrier_semaphore()
    for dev in [at(d, 0) for d in (1, 2, 3)] + [at(0, d) for d in (1, 2, 3)] + [sib]:
        pl.semaphore_signal(barrier, inc=1, device_id=dev, device_id_type=MESH)
    pl.semaphore_wait(barrier, 7)

    def remote(src, dst, s, r, dev):
        return pltpu.make_async_remote_copy(src_ref=src, dst_ref=dst, send_sem=s, recv_sem=r,
                                            device_id=dev, device_id_type=MESH)

    def wait_for(p, sem):
        pltpu.make_async_copy(p, p, sem).wait()

    def rows_of(t):
        return pl.ds(pl.multiple_of(t * 64, 64), 64)

    rows = rows_of(tile)
    LO, HI_, ALL = pl.ds(0, 128), pl.ds(128, 128), pl.ds(0, 256)

    is_s = col != b % 2
    is_w = jnp.logical_not(is_s)
    is_top = tile // 2 == 0
    is_bottom = tile // 2 == 1
    own_slot = jnp.where((b == 1) | (b == 2), 4, 5)

    def first(kind, face, slot, cs, sem):
        dst = g.at[col, slot, rows, cs]
        away = [remote(x_ref.at[(b + d) % 4, face, :, cs], dst, send1.at[kind, d - 1], recv1.at[sem], at(d, 0))
                for d in (1, 3, 2)]
        return away, lambda: pltpu.make_async_copy(x_ref.at[b, face, :, cs], dst, recv1.at[sem])

    def first_a():
        return first(0, col, b // 2, LO, 6 + b // 2)

    def first_b():
        return first(1, col, b // 2, HI_, b // 2)

    def first_w():
        return first(0, 1 - col, 2 + b // 2, ALL, 2 + b // 2)

    def first_own():
        return first(1, col, own_slot, ALL, own_slot)

    def begin(cond, *makers):
        @pl.when(cond)
        def _():
            for maker in makers:
                away, home = maker()
                for c in away:
                    c.start()
                home().start()

    def sent(cond, *makers):
        @pl.when(cond)
        def _():
            for maker in makers:
                for c in maker()[0]:
                    c.wait_send()

    A, B, W = range(3)
    SLOTS = (pl.ds(0, 2), pl.ds(0, 2), pl.ds(2, 3))
    CS = (LO, HI_, ALL)
    SEMS = (((0, 6), (1, 7)), ((0, 0), (1, 1)), ((2, 2), (3, 3), (4, 4)))
    pending = []

    def under(cond, fn):
        if cond is None:
            fn()
        else:
            pl.when(cond)(fn)

    def piece(unit, d, other=0):
        xx = (x + d) % 4
        t = xx % 2 * 2 + core + other * (1 - 2 * core)
        return g.at[xx // 2, SLOTS[unit], rows_of(t), CS[unit]]

    def ring_copy(unit, src, n):
        p = piece(unit, src)
        return remote(p, p, send2.at[unit, n], recv2.at[unit, n], at(0, n) if n in (1, 2, 3) else sib)

    def go(cond, *args):
        ring_copy(*args).start()
        pending.append((cond, args))

    def have(unit, d):
        return None if unit != A else is_top if d % 2 == 0 else is_bottom

    def ring_start(unit):
        cond = have(unit, 0)

        def do():
            for slot, sem in SEMS[unit]:
                wait_for(g.at[col, slot, rows, CS[unit]], recv1.at[sem])
            for d in (2, 1, 3):
                go(cond, unit, 0, d)
            go(cond, unit, 0, 0)
        under(cond, do)

    def ring_share(unit):
        for d in (1, 3, 2):
            cond = have(unit, d)

            def do():
                wait_for(piece(unit, 4 - d), recv2.at[unit, d])
                go(cond, unit, 4 - d, 3 + d)
            under(cond, do)

    def ring_done(unit):
        under(have(unit, 0), lambda: wait_for(piece(unit, 0, 1), recv2.at[unit, 0]))
        for d in (1, 3, 2):
            under(have(unit, d), lambda: wait_for(piece(unit, 4 - d, 1), recv2.at[unit, 3 + d]))

    begin(is_s & is_top, first_a)
    begin(is_s, first_b)
    begin(is_w & is_bottom, first_w, first_own)
    ring_start(A)
    begin(is_w & is_top, first_w, first_own)
    ring_share(A)
    ring_start(B)
    ring_done(A)

    during_first = {3: lambda: ring_start(W), 11: lambda: ring_share(B)}
    during_second = {12: lambda: ring_share(W)}

    def hook(table):
        return lambda k: table[k]() if k in table else None

    for p, a in enumerate((a0, a1)):
        a[0:128, 0:128] = g[0, p, 0:128, 0:128] + g[1, p, 0:128, 0:128]
    factor([a.at[0:128, 0:128] for a in (a0, a1)], [f0, f1], hook(during_first))
    ring_done(B)
    for p, (a, f) in enumerate(((a0, f0), (a1, f1))):
        vy = dot(f[...], g[0, p, 0:128, 128:256] + g[1, p, 0:128, 128:256])
        a[0:128, 0:128] = vy[0:128]
        a[128:256, 128:256] = g[0, p, 128:256, 128:256] + g[1, p, 128:256, 128:256] - dot(vy[0:128], vy[128:], 0, 0)
    factor([a.at[128:256, 128:256] for a in (a0, a1)], [f2, f3], hook(during_second))
    ring_done(W)
    for p, a in enumerate((a0, a1)):
        a[:, 256:512] = g[0, 2 + p]
        a[:, 512:768] = g[1, 2 + p]
    for a, f, h, v, y in ((a0, f0, f2, v0, y0), (a1, f1, f3, v1, y1)):
        vy = dot(f[...], a[0:128, 256:])
        v[0:128, :] = vy[0:128]
        y[0:128, :] = vy[128:]
        vy = dot(h[...], a[128:256, 256:] - dot(a[0:128, 0:128], vy[128:], 0, 0))
        v[128:256, :] = vy[0:128]
        y[128:256, :] = vy[128:]

    p0 = dot(v0[:, 256:512], y0[...], 0, 0)
    p1 = dot(v1[:, 0:256], y1[...], 0, 0)
    a2[:, 0:256] = g[0, 4] + g[1, 4] - p0[:, 256:512] - p1[:, 0:256]
    a2[:, 256:512] = -p0[:, 0:256]
    a2[:, 512:768] = -p1[:, 256:512]
    solve(a2, f0, v2, y2)

    start = pl.multiple_of(tile // 2 * 128, 128)
    cols = pl.multiple_of(col * 256, 256)
    a0[:, 0:128] = v2[:, pl.ds(start, 128)]
    a0[:, 128:256] = v2[:, pl.ds(start + 256, 128)]
    a0[:, 256:512] = y2[:, pl.ds(cols, 256)]
    a1[:, 0:128] = jnp.where(col == 0, v0[:, pl.ds(start, 128)], v1[:, pl.ds(start + 256, 128)])
    a1[:, 256:512] = jnp.where(col == 0, y0[:, 0:256], y1[:, 256:512])
    a2[:, 0:256] = dot(a0[:, 0:256], a0[:, 256:512], 0, 0)
    a2[0:128, 256:512] = dot(a1[:, 0:128], a1[:, 256:512], 0, 0)
    row = pl.multiple_of(core * 64, 64)
    wait_for(g.at[col, 5, rows, :], recv1.at[5])
    own = g[col, 5, rows, :] - a2[pl.ds(row, 64), 256:512]
    ob[0:64, :] = jnp.where(col == 0, own, 0.0) - a2[pl.ds(row, 64), 0:256]
    ob[64:128, :] = jnp.where(col == 1, own, 0.0) - a2[pl.ds(128 + row, 64), 0:256]

    def result(to):
        return ob.at[pl.ds(pl.multiple_of(to * 32, 32), 32), :]

    outs = [remote(result((b + d) % 4), out_ref.at[b], sendo.at[d - 1], recvo.at[d - 1], at(d, 0)) for d in (1, 2, 3)]
    for c in outs:
        c.start()
    home = pltpu.make_async_copy(result(b), out_ref.at[b], recvo.at[3])
    home.start()
    for c in outs:
        c.wait_send()
    for d in (1, 2, 3):
        wait_for(out_ref.at[(b + 4 - d) % 4], recvo.at[d - 1])
    home.wait()
    for cond in (None, is_top, is_bottom):
        def drain():
            for c, args in pending:
                if c is cond:
                    ring_copy(*args).wait_send()
        under(cond, drain)
    sent(is_s & is_top, first_a)
    sent(is_s, first_b)
    sent(is_w, first_w, first_own)


def per_device(box_operators):
    V = pltpu.VMEM
    f = jnp.float32
    dma = pltpu.SemaphoreType.DMA
    out = pl.pallas_call(
        kernel,
        out_shape=jax.ShapeDtypeStruct((4, 32, 256), f),
        in_specs=[pl.BlockSpec(memory_space=pl.ANY)],
        out_specs=pl.BlockSpec(memory_space=pl.ANY),
        scratch_shapes=[V((2, 6, 256, 256), f), V((128, 256), f)] + [V((256, 768), f)] * 3 + [V((256, 512), f)] * 6
        + [V((256, 128), f)] * 4
        + [dma((2, 3)), dma((8,)), dma((3, 7)), dma((3, 7)), dma((3,)), dma((4,))],
        compiler_params=pltpu.CompilerParams(vmem_limit_bytes=40 << 20, collective_id=0, has_side_effects=True),
    )(box_operators[:, 0])
    return out[:, None]


def solution(mesh):
    return jax.shard_map(
        per_device,
        mesh=mesh,
        in_specs=(P(None, "box", None, "tile", "col"),),
        out_specs=P(None, "box", "tile", "col"),
        check_vma=False,
    )
```

time: 158 us -> 56.6 us (0.36)
  waiting for transfers between devices: 96.3 us -> 0 us
  Pallas kernels: 27 us -> 54.7 us
  between operations: 13.5 us -> 0.01 us
  blocking collectives: 9.41 us -> 0 us
  starting transfers between devices: 7.85 us -> 0 us
    all_gather x2 -> x0, waiting for transfers between devices: 83.1 us -> none  [the longest x1 51 us: per_device(): g = lax.all_gather(g, 'col', axis=0)]
    pallas_call x1, Pallas kernels: 27 us -> 54.7 us  [per_device(): pl.pallas_call(kernel, out_shape=jax.ShapeDtypeStruct((4, 32, 256), f), i...]
    all_to_all x1 -> x0, waiting for transfers between devices: 13.1 us -> none  [per_device(): parts = lax.all_to_all(x, 'box', 0, 0, axis_index_groups=groups, tiled=True)]
    all_to_all x1 -> x0, blocking collectives: 9.41 us -> none  [per_device(): out = lax.all_to_all(out, 'box', 0, 0, axis_index_groups=groups, tiled=True)]
    all_to_all x1 -> x0, starting transfers between devices: 7.81 us -> none  [per_device(): parts = lax.all_to_all(x, 'box', 0, 0, axis_index_groups=groups, tiled=True)]
  transfers between devices with their start and end apart: 3 -> 0, of which waited for: 3 -> 0; matrix products, arithmetic and copies ran while one was open for 0% -> 0% of each run, Pallas kernels for 0% -> 0%
where the time goes in v3:
time: 56.6 us; the launch traced here: 56.4 us
  Pallas kernels  54.7 us (97%)
  local copies, waits for them, and re-layouts  1.7 us (3%)
    pallas_call x1, Pallas kernels, per_device(): pl.pallas_call(kernel, out_shape=jax.ShapeDtypeStruct((4, 32, 256), f), i...  54.7 us
    unnamed x3, local copies, waits for them, and re-layouts  1.7 us

profile of v3, /device:TPU:1, one launch (start us, length us, event | category | flops | bytes accessed | tf_op | source)
XLA Modules:
  0.0 56.4 jit_solution(452240357458707991)
XLA Ops:
  0.0 0.0 copy-start
  0.0 1.0 %copy-done = f32[4,1,2,64,256]{4,3,2,1,0:T(8,128)S(1)} copy-done((f32[4,1,2,64,256]{4,3,2,1,0:T(8,128)S(1)}, f32[4,1,2,64,256]{4,3,2,1,0:T(8,128)}, u32[]{:S(2)}) %copy-start) | copy-done | bytes 524312
  1.0 54.7 %shard_map.17 = f32[4,32,256]{2,1,0:T(8,128)S(1)} custom-call(f32[4,2,64,256]{3,2,1,0:T(8,128)S(1)} %bitcast.4), custom_call_target="tpu_custom_call" | custom-call | tf_op jit(solution)/shard_map/pallas_call | solution.py:295
  55.8 0.7 %copy.4 = f32[4,1,32,256]{3,2,1,0:T(8,128)} copy(f32[4,1,32,256]{3,2,1,0:T(8,128)S(1)} %bitcast.5) | data formatting | bytes 262144
Async XLA Ops:
  0.0 1.0 %copy-start = (f32[4,1,2,64,256]{4,3,2,1,0:T(8,128)S(1)}, f32[4,1,2,64,256]{4,3,2,1,0:T(8,128)}, u32[]{:S(2)}) copy-start(f32[4,1,2,64,256]{4,3,2,1,0:T(8,128)} %param.1) | copy-start | bytes 1572868

commit v4 on v3

--- a/solution.py
+++ b/solution.py
@@ -12,17 +12,18 @@
 
 def leaf(cols, sub):
     cols = list(cols)
+    scale = None
     for k in range(8):
-        piv = 1.0 / jnp.broadcast_to(cols[k][k:k+1, :], (8, 128))
+        piv = 1.0 / jnp.broadcast_to(cols[k][k:k + 1, :], (8, 128))
         here = sub == k
-        ck = cols[k]
-        for c in range(8):
-            if c == k:
-                continue
-            row = jnp.broadcast_to(cols[c][k:k+1, :], (8, 128)) * piv
-            cols[c] = jnp.where(here, row, cols[c] - ck * row)
-        cols[k] = jnp.where(here, piv, -ck * piv)
-    return cols
+        factors = jnp.where(here, 0.0, cols[k]) * piv
+        scale = piv if scale is None else jnp.where(sub >= k, piv, scale)
+        for q in range(1, 8):
+            c = (k + q) % 8
+            cols[c] = cols[c] - factors * jnp.broadcast_to(cols[c][k:k + 1, :], (8, 128))
+        cols[k] = jnp.where(here, 1.0, -factors)
+    return [c * scale for c in cols]
+
 
 def treesum(xs):
     while len(xs) > 1:
@@ -31,32 +32,50 @@
 
 def apply8(cols, y):
     return treesum([cols[j] * jnp.broadcast_to(y[j:j+1, :], (8, 128)) for j in range(8)])
+
+PANEL = 4
+LOOK = 2
+
 
 def eliminate(mats, hook=None):
     sub = lax.broadcasted_iota(jnp.int32, (8, 128), 0)
     lane = lax.broadcasted_iota(jnp.int32, (8, 128), 1)
     mats = [list(m) for m in mats]
     es = [[] for _ in mats]
-    des = [[] for _ in mats]
+    fs = [[] for _ in mats]
+    panels = [[] for _ in mats]
     for k in range(16):
         if hook is not None:
             hook(k)
         lo = 8 * k
-        inblk = (lane >= lo) & (lane < lo + 8)
+        end = k // PANEL * PANEL + PANEL
+        inside = (lane >= lo) & (lane < lo + 8)
         eye = jnp.where(lane == sub + lo, 1.0, 0.0).astype(jnp.float32)
         for n, m in enumerate(mats):
             r = m[k]
-            cols = leaf([jnp.broadcast_to(r[:, lo+c:lo+c+1], (8, 128)) for c in range(8)], sub)
-            rm = jnp.where(inblk, eye, r)
+            cols = leaf([jnp.broadcast_to(r[:, lo + c:lo + c + 1], (8, 128)) for c in range(8)], sub)
+            rm = jnp.where(inside, eye, r)
             y = apply8(cols, rm)
             es[n].append(jnp.where(lane < lo + 8, rm, 0.0))
-            des[n].append(jnp.where(lane < lo + 8, y, 0.0))
-            ys = [jnp.broadcast_to(y[j:j+1, :], (8, 128)) for j in range(8)]
-            for i in range(k + 1, 16):
+            fs[n].append(jnp.where(lane < lo + 8, y, 0.0))
+            panels[n].append((rm, jnp.where((lane >= lo + 8) & (lane < 8 * end), 0.0, y)))
+            yb = [jnp.broadcast_to(y[j:j + 1, :], (8, 128)) for j in range(8)]
+            for i in range(k + 1, min(end + LOOK, 16)):
                 a = m[i]
-                upd = treesum([jnp.broadcast_to(a[:, lo+j:lo+j+1], (8, 128)) * ys[j] for j in range(8)])
-                m[i] = jnp.where(inblk, 0.0, a) - upd
-    return es, des
+                m[i] = jnp.where(inside, 0.0, a) - treesum(
+                    [jnp.broadcast_to(a[:, lo + j:lo + j + 1], (8, 128)) * yb[j] for j in range(8)])
+        if k + 1 == end and end + LOOK < 16:
+            gone = (lane >= 8 * (end - PANEL)) & (lane < 8 * end)
+            for n, m in enumerate(mats):
+                v = jnp.concatenate([p[0] for p in panels[n]], axis=0)
+                y = jnp.concatenate([p[1] for p in panels[n]], axis=0)
+                update = dot(v, y, 0, 0)
+                for i in range(end + LOOK, 16):
+                    m[i] = jnp.where(gone, 0.0, m[i]) - update[8 * i:8 * i + 8, :]
+        if k + 1 == end:
+            panels = [[] for _ in mats]
+    return es, fs
+
 
 def factor(mat_refs, fac_refs, hook=None):
     es, des = eliminate([[m[8*i:8*i+8, :] for i in range(16)] for m in mat_refs], hook)
@@ -64,6 +83,17 @@
         for i in range(16):
             f[8*i:8*i+8, :] = e[i]
             f[128+8*i:128+8*i+8, :] = d[i]
+
+def dot3(a, b, ca=1, cb=0):
+    ah = a.astype(jnp.bfloat16)
+    al = (a - ah.astype(jnp.float32)).astype(jnp.bfloat16)
+    bh = b.astype(jnp.bfloat16)
+    bl = (b - bh.astype(jnp.float32)).astype(jnp.bfloat16)
+
+    def one(p, q):
+        return lax.dot_general(p, q, (((ca,), (cb,)), ((), ())), preferred_element_type=jnp.float32)
+    return one(ah, bh) + (one(ah, bl) + one(al, bh))
+
 
 def solve(a, fac, v, y):
     factor([a.at[0:128, 0:128]], [fac])
@@ -214,9 +244,10 @@
     ring_share(A)
     ring_start(B)
     ring_done(A)
-
-    during_first = {3: lambda: ring_start(W), 11: lambda: ring_share(B)}
-    during_second = {12: lambda: ring_share(W)}
+    ring_start(W)
+
+    during_first = {}
+    during_second = {}
 
     def hook(table):
         return lambda k: table[k]() if k in table else None
@@ -224,26 +255,28 @@
     for p, a in enumerate((a0, a1)):
         a[0:128, 0:128] = g[0, p, 0:128, 0:128] + g[1, p, 0:128, 0:128]
     factor([a.at[0:128, 0:128] for a in (a0, a1)], [f0, f1], hook(during_first))
+    ring_share(B)
     ring_done(B)
     for p, (a, f) in enumerate(((a0, f0), (a1, f1))):
         vy = dot(f[...], g[0, p, 0:128, 128:256] + g[1, p, 0:128, 128:256])
         a[0:128, 0:128] = vy[0:128]
         a[128:256, 128:256] = g[0, p, 128:256, 128:256] + g[1, p, 128:256, 128:256] - dot(vy[0:128], vy[128:], 0, 0)
     factor([a.at[128:256, 128:256] for a in (a0, a1)], [f2, f3], hook(during_second))
+    ring_share(W)
     ring_done(W)
     for p, a in enumerate((a0, a1)):
         a[:, 256:512] = g[0, 2 + p]
         a[:, 512:768] = g[1, 2 + p]
     for a, f, h, v, y in ((a0, f0, f2, v0, y0), (a1, f1, f3, v1, y1)):
-        vy = dot(f[...], a[0:128, 256:])
+        vy = dot3(f[...], a[0:128, 256:])
         v[0:128, :] = vy[0:128]
         y[0:128, :] = vy[128:]
-        vy = dot(h[...], a[128:256, 256:] - dot(a[0:128, 0:128], vy[128:], 0, 0))
+        vy = dot3(h[...], a[128:256, 256:] - dot3(a[0:128, 0:128], vy[128:], 0, 0))
         v[128:256, :] = vy[0:128]
         y[128:256, :] = vy[128:]
 
-    p0 = dot(v0[:, 256:512], y0[...], 0, 0)
-    p1 = dot(v1[:, 0:256], y1[...], 0, 0)
+    p0 = dot3(v0[:, 256:512], y0[...], 0, 0)
+    p1 = dot3(v1[:, 0:256], y1[...], 0, 0)
     a2[:, 0:256] = g[0, 4] + g[1, 4] - p0[:, 256:512] - p1[:, 0:256]
     a2[:, 256:512] = -p0[:, 0:256]
     a2[:, 512:768] = -p1[:, 256:512]
@@ -256,8 +289,8 @@
     a0[:, 256:512] = y2[:, pl.ds(cols, 256)]
     a1[:, 0:128] = jnp.where(col == 0, v0[:, pl.ds(start, 128)], v1[:, pl.ds(start + 256, 128)])
     a1[:, 256:512] = jnp.where(col == 0, y0[:, 0:256], y1[:, 256:512])
-    a2[:, 0:256] = dot(a0[:, 0:256], a0[:, 256:512], 0, 0)
-    a2[0:128, 256:512] = dot(a1[:, 0:128], a1[:, 256:512], 0, 0)
+    a2[:, 0:256] = dot3(a0[:, 0:256], a0[:, 256:512], 0, 0)
+    a2[0:128, 256:512] = dot3(a1[:, 0:128], a1[:, 256:512], 0, 0)
     row = pl.multiple_of(core * 64, 64)
     wait_for(g.at[col, 5, rows, :], recv1.at[5])
     own = g[col, 5, rows, :] - a2[pl.ds(row, 64), 256:512]

time: 56.6 us -> 51.9 us (0.917); the launches traced: 56.4 us -> 51.1 us
  Pallas kernels: 54.7 us -> 49.4 us
    pallas_call x1, Pallas kernels: 54.7 us -> 49.4 us  [per_device(): pl.pallas_call(kernel, out_shape=jax.ShapeDtypeStruct((4, 32, 256), f), i...]
where the time goes in v4:
time: 51.9 us; the launch traced here: 51.1 us
  Pallas kernels  49.4 us (95%)
  local copies, waits for them, and re-layouts  1.7 us (3%)
    pallas_call x1, Pallas kernels, per_device(): pl.pallas_call(kernel, out_shape=jax.ShapeDtypeStruct((4, 32, 256), f), i...  49.4 us
    unnamed x3, local copies, waits for them, and re-layouts  1.7 us

profile of v4, /device:TPU:1, one launch (start us, length us, event | category | flops | bytes accessed | tf_op | source)
XLA Modules:
  0.0 51.1 jit_solution(16405577906610821818)
XLA Ops:
  0.0 0.0 copy-start
  0.0 1.0 %copy-done = f32[4,1,2,64,256]{4,3,2,1,0:T(8,128)S(1)} copy-done((f32[4,1,2,64,256]{4,3,2,1,0:T(8,128)S(1)}, f32[4,1,2,64,256]{4,3,2,1,0:T(8,128)}, u32[]{:S(2)}) %copy-start) | copy-done | bytes 524312
  1.0 49.4 %shard_map.17 = f32[4,32,256]{2,1,0:T(8,128)S(1)} custom-call(f32[4,2,64,256]{3,2,1,0:T(8,128)S(1)} %bitcast.4), custom_call_target="tpu_custom_call" | custom-call | tf_op jit(solution)/shard_map/pallas_call | solution.py:328
  50.4 0.7 %copy.4 = f32[4,1,32,256]{3,2,1,0:T(8,128)} copy(f32[4,1,32,256]{3,2,1,0:T(8,128)S(1)} %bitcast.5) | data formatting | bytes 262144
Async XLA Ops:
  0.0 1.0 %copy-start = (f32[4,1,2,64,256]{4,3,2,1,0:T(8,128)S(1)}, f32[4,1,2,64,256]{4,3,2,1,0:T(8,128)}, u32[]{:S(2)}) copy-start(f32[4,1,2,64,256]{4,3,2,1,0:T(8,128)} %param.1) | copy-start | bytes 1572868

commit v5 on v4

--- a/solution.py
+++ b/solution.py
@@ -95,21 +95,23 @@
     return one(ah, bh) + (one(ah, bl) + one(al, bh))
 
 
-def solve(a, fac, v, y):
+def solve(a, fac, fac2, v, y):
     factor([a.at[0:128, 0:128]], [fac])
-    vy = dot(fac[...], a[0:128, 128:])
-    v[0:128, :] = vy[0:128, 128:]
-    y[0:128, :] = vy[128:, 128:]
-    a[128:256, 128:] = a[128:256, 128:] - dot(vy[0:128, 0:128], vy[128:, :], 0, 0)
-    factor([a.at[128:256, 128:256]], [fac])
-    vy = dot(fac[...], a[128:256, 256:])
-    v[128:256, :] = vy[0:128, :]
-    y[128:256, :] = vy[128:, :]
+    vy = dot(fac[...], a[0:128, 128:256])
+    a[128:256, 128:256] = a[128:256, 128:256] - dot(vy[0:128], vy[128:], 0, 0)
+    wide = dot3(fac[...], a[0:128, 256:])
+    v[0:128, :] = wide[0:128]
+    y[0:128, :] = wide[128:]
+    a[128:256, 256:] = a[128:256, 256:] - dot3(vy[0:128], wide[128:], 0, 0)
+    factor([a.at[128:256, 128:256]], [fac2])
+    wide = dot3(fac2[...], a[128:256, 256:])
+    v[128:256, :] = wide[0:128]
+    y[128:256, :] = wide[128:]
 
 
 MESH = pl.DeviceIdType.MESH
 
-def kernel(x_ref, out_ref, g, ob, a0, a1, a2, v0, v1, v2, y0, y1, y2, f0, f1, f2, f3,
+def kernel(x_ref, out_ref, g, ob, a0, a1, a2, v0, v1, v2, y0, y1, y2, f0, f1, f2, f3, e0, e1,
            send1, recv1, send2, recv2, sendo, recvo):
     box = lax.axis_index("box")
     tile = lax.axis_index("tile")
@@ -222,8 +224,8 @@
             go(cond, unit, 0, 0)
         under(cond, do)
 
-    def ring_share(unit):
-        for d in (1, 3, 2):
+    def ring_share(unit, ds=(1, 3, 2)):
+        for d in ds:
             cond = have(unit, d)
 
             def do():
@@ -263,37 +265,42 @@
         a[128:256, 128:256] = g[0, p, 128:256, 128:256] + g[1, p, 128:256, 128:256] - dot(vy[0:128], vy[128:], 0, 0)
     factor([a.at[128:256, 128:256] for a in (a0, a1)], [f2, f3], hook(during_second))
     ring_share(W)
+    for a, f, h, ef in ((a0, f0, f2, e0), (a1, f1, f3, e1)):
+        low = dot3(h[...], -dot3(a[0:128, 0:128], f[128:256, :], 0, 0))
+        ef[0:128, 0:128] = f[0:128, :]
+        ef[0:128, 128:256] = jnp.zeros((128, 128), jnp.float32)
+        ef[128:256, 0:128] = low[0:128]
+        ef[128:256, 128:256] = h[0:128, :]
+        ef[256:384, 0:128] = f[128:256, :]
+        ef[256:384, 128:256] = jnp.zeros((128, 128), jnp.float32)
+        ef[384:512, 0:128] = low[128:]
+        ef[384:512, 128:256] = h[128:256, :]
     ring_done(W)
-    for p, a in enumerate((a0, a1)):
-        a[:, 256:512] = g[0, 2 + p]
-        a[:, 512:768] = g[1, 2 + p]
-    for a, f, h, v, y in ((a0, f0, f2, v0, y0), (a1, f1, f3, v1, y1)):
-        vy = dot3(f[...], a[0:128, 256:])
-        v[0:128, :] = vy[0:128]
-        y[0:128, :] = vy[128:]
-        vy = dot3(h[...], a[128:256, 256:] - dot3(a[0:128, 0:128], vy[128:], 0, 0))
-        v[128:256, :] = vy[0:128]
-        y[128:256, :] = vy[128:]
-
-    p0 = dot3(v0[:, 256:512], y0[...], 0, 0)
-    p1 = dot3(v1[:, 0:256], y1[...], 0, 0)
-    a2[:, 0:256] = g[0, 4] + g[1, 4] - p0[:, 256:512] - p1[:, 0:256]
-    a2[:, 256:512] = -p0[:, 0:256]
-    a2[:, 512:768] = -p1[:, 256:512]
-    solve(a2, f0, v2, y2)
+    for p, (ef, v, y) in enumerate(((e0, v0, y0), (e1, v1, y1))):
+        for c in (1 - p, p):
+            vy = dot3(ef[...], g[c, 2 + p])
+            v[:, 256 * c:256 * c + 256] = vy[0:256]
+            y[:, 256 * c:256 * c + 256] = vy[256:512]
+
+    a2[:, 0:256] = (g[0, 4] + g[1, 4] - dot3(v0[:, 256:512], y0[:, 256:512], 0, 0)
+                    - dot3(v1[:, 0:256], y1[:, 0:256], 0, 0))
+    a2[:, 256:512] = -dot3(v0[:, 256:512], y0[:, 0:256], 0, 0)
+    a2[:, 512:768] = -dot3(v1[:, 0:256], y1[:, 256:512], 0, 0)
 
     start = pl.multiple_of(tile // 2 * 128, 128)
     cols = pl.multiple_of(col * 256, 256)
+    a1[:, 0:128] = jnp.where(col == 0, v0[:, pl.ds(start, 128)], v1[:, pl.ds(start + 256, 128)])
+    a1[:, 256:512] = jnp.where(col == 0, y0[:, 0:256], y1[:, 256:512])
+    a0[0:128, 512:768] = dot3(a1[:, 0:128], a1[:, 256:512], 0, 0)
+    solve(a2, f0, f1, v2, y2)
+
     a0[:, 0:128] = v2[:, pl.ds(start, 128)]
     a0[:, 128:256] = v2[:, pl.ds(start + 256, 128)]
     a0[:, 256:512] = y2[:, pl.ds(cols, 256)]
-    a1[:, 0:128] = jnp.where(col == 0, v0[:, pl.ds(start, 128)], v1[:, pl.ds(start + 256, 128)])
-    a1[:, 256:512] = jnp.where(col == 0, y0[:, 0:256], y1[:, 256:512])
     a2[:, 0:256] = dot3(a0[:, 0:256], a0[:, 256:512], 0, 0)
-    a2[0:128, 256:512] = dot3(a1[:, 0:128], a1[:, 256:512], 0, 0)
     row = pl.multiple_of(core * 64, 64)
     wait_for(g.at[col, 5, rows, :], recv1.at[5])
-    own = g[col, 5, rows, :] - a2[pl.ds(row, 64), 256:512]
+    own = g[col, 5, rows, :] - a0[pl.ds(row, 64), 512:768]
     ob[0:64, :] = jnp.where(col == 0, own, 0.0) - a2[pl.ds(row, 64), 0:256]
     ob[64:128, :] = jnp.where(col == 1, own, 0.0) - a2[pl.ds(128 + row, 64), 0:256]
 
@@ -331,7 +338,7 @@
         in_specs=[pl.BlockSpec(memory_space=pl.ANY)],
         out_specs=pl.BlockSpec(memory_space=pl.ANY),
         scratch_shapes=[V((2, 6, 256, 256), f), V((128, 256), f)] + [V((256, 768), f)] * 3 + [V((256, 512), f)] * 6
-        + [V((256, 128), f)] * 4
+        + [V((256, 128), f)] * 4 + [V((512, 256), f)] * 2
         + [dma((2, 3)), dma((8,)), dma((3, 7)), dma((3, 7)), dma((3,)), dma((4,))],
         compiler_params=pltpu.CompilerParams(vmem_limit_bytes=40 << 20, collective_id=0, has_side_effects=True),
     )(box_operators[:, 0])

time: 51.9 us -> 51 us (0.983)
  Pallas kernels: 49.4 us -> 48.5 us
    pallas_call x1, Pallas kernels: 49.4 us -> 48.5 us  [per_device(): pl.pallas_call(kernel, out_shape=jax.ShapeDtypeStruct((4, 32, 256), f), i...]
where the time goes in v5:
time: 51 us; the launch traced here: 50.2 us
  Pallas kernels  48.5 us (95%)
  local copies, waits for them, and re-layouts  1.7 us (3%)
    pallas_call x1, Pallas kernels, per_device(): pl.pallas_call(kernel, out_shape=jax.ShapeDtypeStruct((4, 32, 256), f), i...  48.5 us
    unnamed x3, local copies, waits for them, and re-layouts  1.7 us

profile of v5, /device:TPU:1, one launch (start us, length us, event | category | flops | bytes accessed | tf_op | source)
XLA Modules:
  0.0 50.2 jit_solution(897666116369093397)
XLA Ops:
  0.0 0.0 copy-start
  0.0 1.0 %copy-done = f32[4,1,2,64,256]{4,3,2,1,0:T(8,128)S(1)} copy-done((f32[4,1,2,64,256]{4,3,2,1,0:T(8,128)S(1)}, f32[4,1,2,64,256]{4,3,2,1,0:T(8,128)}, u32[]{:S(2)}) %copy-start) | copy-done | bytes 524312
  1.0 48.5 %shard_map.17 = f32[4,32,256]{2,1,0:T(8,128)S(1)} custom-call(f32[4,2,64,256]{3,2,1,0:T(8,128)S(1)} %bitcast.4), custom_call_target="tpu_custom_call" | custom-call | tf_op jit(solution)/shard_map/pallas_call | solution.py:335
  49.5 0.7 %copy.4 = f32[4,1,32,256]{3,2,1,0:T(8,128)} copy(f32[4,1,32,256]{3,2,1,0:T(8,128)S(1)} %bitcast.5) | data formatting | bytes 262144
Async XLA Ops:
  0.0 1.0 %copy-start = (f32[4,1,2,64,256]{4,3,2,1,0:T(8,128)S(1)}, f32[4,1,2,64,256]{4,3,2,1,0:T(8,128)}, u32[]{:S(2)}) copy-start(f32[4,1,2,64,256]{4,3,2,1,0:T(8,128)} %param.1) | copy-start | bytes 1572868

commit v6 on v5

--- a/solution.py
+++ b/solution.py
@@ -40,6 +40,7 @@
 def eliminate(mats, hook=None):
     sub = lax.broadcasted_iota(jnp.int32, (8, 128), 0)
     lane = lax.broadcasted_iota(jnp.int32, (8, 128), 1)
+    panel = PANEL if len(mats) > 1 else PANEL // 2
     mats = [list(m) for m in mats]
     es = [[] for _ in mats]
     fs = [[] for _ in mats]
@@ -48,7 +49,7 @@
         if hook is not None:
             hook(k)
         lo = 8 * k
-        end = k // PANEL * PANEL + PANEL
+        end = k // panel * panel + panel
         inside = (lane >= lo) & (lane < lo + 8)
         eye = jnp.where(lane == sub + lo, 1.0, 0.0).astype(jnp.float32)
         for n, m in enumerate(mats):
@@ -65,7 +66,7 @@
                 m[i] = jnp.where(inside, 0.0, a) - treesum(
                     [jnp.broadcast_to(a[:, lo + j:lo + j + 1], (8, 128)) * yb[j] for j in range(8)])
         if k + 1 == end and end + LOOK < 16:
-            gone = (lane >= 8 * (end - PANEL)) & (lane < 8 * end)
+            gone = (lane >= 8 * (end - panel)) & (lane < 8 * end)
             for n, m in enumerate(mats):
                 v = jnp.concatenate([p[0] for p in panels[n]], axis=0)
                 y = jnp.concatenate([p[1] for p in panels[n]], axis=0)

time: 51 us -> 50.6 us (level)
  no operation moved by 1% of the time
where the time goes in v6:
time: 50.6 us; the launch traced here: 49.8 us
  Pallas kernels  48.1 us (95%)
  local copies, waits for them, and re-layouts  1.7 us (3%)
    pallas_call x1, Pallas kernels, per_device(): pl.pallas_call(kernel, out_shape=jax.ShapeDtypeStruct((4, 32, 256), f), i...  48.1 us
    unnamed x3, local copies, waits for them, and re-layouts  1.7 us

profile of v6, /device:TPU:1, one launch (start us, length us, event | category | flops | bytes accessed | tf_op | source)
XLA Modules:
  0.0 49.8 jit_solution(17136428368305688449)
XLA Ops:
  0.0 0.0 copy-start
  0.0 1.0 %copy-done = f32[4,1,2,64,256]{4,3,2,1,0:T(8,128)S(1)} copy-done((f32[4,1,2,64,256]{4,3,2,1,0:T(8,128)S(1)}, f32[4,1,2,64,256]{4,3,2,1,0:T(8,128)}, u32[]{:S(2)}) %copy-start) | copy-done | bytes 524312
  1.0 48.1 %shard_map.17 = f32[4,32,256]{2,1,0:T(8,128)S(1)} custom-call(f32[4,2,64,256]{3,2,1,0:T(8,128)S(1)} %bitcast.4), custom_call_target="tpu_custom_call" | custom-call | tf_op jit(solution)/shard_map/pallas_call | solution.py:336
  49.1 0.7 %copy.4 = f32[4,1,32,256]{3,2,1,0:T(8,128)} copy(f32[4,1,32,256]{3,2,1,0:T(8,128)S(1)} %bitcast.5) | data formatting | bytes 262144
Async XLA Ops:
  0.0 1.0 %copy-start = (f32[4,1,2,64,256]{4,3,2,1,0:T(8,128)S(1)}, f32[4,1,2,64,256]{4,3,2,1,0:T(8,128)}, u32[]{:S(2)}) copy-start(f32[4,1,2,64,256]{4,3,2,1,0:T(8,128)} %param.1) | copy-start | bytes 1572868
